TPU v7x, 256 devices: a whole 4x4x8 slice. The times are simulated.
256 devices in a mesh: group: 4 (over x), leaf: 64 (over z, y, core).
Axes of the slice: x: 4, y: 4, z: 8, core: 2. Of those that a mesh axis runs over, the one named last changes fastest.
Arguments:
- right_sides: float32 [16, 1048576], P(None, ('group', 'leaf')), may hold values from -6 to 6
- near_blocks: float32 [16384, 8, 4096], P(('group', 'leaf')), may hold values from -0.375 to 0.375
- near_source: int32 [16384, 8], P(('group', 'leaf')), may hold values from 0 to 16383, as said below
- near_count: int32 [16384], P(('group', 'leaf')), may hold values from 1 to 8
- basis: float32 [16384, 2048], P(('group', 'leaf')), may hold values from -0.75 to 0.75
- leaf_source: int32 [16384, 8], P(('group', 'leaf')), may hold values from 0 to 16383
- leaf_coupling: float32 [16384, 8, 1024], P(('group', 'leaf')), may hold values from -0.375 to 0.375
- leaf_transfer: float32 [16384, 1024], P(('group', 'leaf')), may hold values from -1 to 1
- cluster_source: int32 [1024, 8], P(('group', 'leaf')), may hold values from 0 to 255
- cluster_coupling: float32 [1024, 8, 1024], P(('group', 'leaf')), may hold values from -0.09375 to 0.09375
- cluster_transfer: float32 [1024, 1024], P(('group', 'leaf')), may hold values from -1 to 1
- group_coupling: float32 [4, 4, 1024], P('group'), may hold values from -0.0078125 to 0.0078125
Outputs:
- applied: float32 [16, 1048576], P(None, ('group', 'leaf'))
Inputs may be any that keep to these rules, and one draw needn't show every extreme that they name: near_source[t, j] and leaf_source[t, j] name a leaf held by the same device as t or by the device just before or after it in the order of devices.
All inputs are finite; a program needn't handle non-finite values.
Results may differ from a plain program's by a relative error of at most 0.0001.
Values sent between devices are 32-bit elements; how exact they have to be, the bound alone decides.
No kernel may reach another device: no remote copies, remote signals or barrier semaphores. Data moves between devices by JAX's collectives and lax.ppermute only.
A program may use at most 128 MiB of HBM per device.

v0:
```python
import jax
import jax.numpy as jnp
from jax import lax
from jax.sharding import PartitionSpec as P

LEAF = 64
K = 32
RHS = 16
FAR0 = 8
FAR1 = 8
highest_precision = lax.Precision.HIGHEST


def extended(value, sides, width):
    for axis, dim in sides:
        size, length = (lax.axis_size(axis), value.shape[dim])
        up = [(i, (i + 1) % size) for i in range(size - 1)]
        down = [(j, i) for i, j in up]
        last = lax.slice_in_dim(value, length - width, length, axis=dim)
        leading = lax.slice_in_dim(value, 0, width, axis=dim)
        before = lax.ppermute(last, axis, up)
        after = lax.ppermute(leading, axis, down)
        value = jnp.concatenate([before, value, after], axis=dim)
    return value


def per_device(
    right_sides,
    near_blocks,
    near_source,
    near_count,
    basis,
    leaf_source,
    leaf_coupling,
    leaf_transfer,
    cluster_source,
    cluster_coupling,
    cluster_transfer,
    group_coupling,
):
    leaves_here = near_blocks.shape[0]
    clusters_here = cluster_coupling.shape[0]
    ngroups = lax.axis_size("group")
    device = lax.axis_index(("group", "leaf"))
    blocks = right_sides.reshape(RHS, leaves_here, LEAF).transpose(1, 0, 2)
    bases = basis.reshape(leaves_here, K, LEAF)
    leaf_coef = jnp.einsum("tka,tra->tkr", bases, blocks, precision=highest_precision)
    coef_rows = leaf_coef.transpose(2, 0, 1).reshape(RHS, leaves_here * K)
    point_ext = extended(right_sides, ((("group", "leaf"), 1),), leaves_here * LEAF)
    coef_ext = extended(coef_rows, ((("group", "leaf"), 1),), leaves_here * K)
    window_start = (device - 1) * leaves_here
    near_local = near_source - window_start
    point_blocks = point_ext.reshape(RHS, 3 * leaves_here, LEAF).transpose(1, 0, 2)
    busiest = jnp.max(near_count)

    def near_step(slot_index, running):
        picked = jnp.take(point_blocks, near_local[:, slot_index], axis=0)
        slab = lax.dynamic_index_in_dim(near_blocks, slot_index, axis=1, keepdims=False).reshape(
            leaves_here, LEAF, LEAF
        )
        live = (near_count > slot_index).astype(jnp.float32)
        term = jnp.einsum("tab,trb->tra", slab, picked, precision=highest_precision)
        return running + term * live[:, None, None]

    near_total = lax.fori_loop(
        0, busiest, near_step, jnp.zeros((leaves_here, RHS, LEAF), jnp.float32)
    )
    coef_blocks = coef_ext.reshape(RHS, 3 * leaves_here, K)
    picked_coef = jnp.take(coef_blocks, leaf_source - window_start, axis=1)
    leaf_far = jnp.einsum(
        "tjkl,rtjl->tkr",
        leaf_coupling.reshape(leaves_here, FAR0, K, K),
        picked_coef,
        precision=highest_precision,
    )
    transfers = leaf_transfer.reshape(leaves_here, K, K)
    lifted = jnp.einsum("tkl,tlr->tkr", transfers, leaf_coef, precision=highest_precision)
    cluster_coef = lifted.reshape(clusters_here, leaves_here // clusters_here, K, RHS).sum(axis=1)
    cluster_rows = cluster_coef.reshape(clusters_here, K * RHS)
    couplings = cluster_coupling.reshape(clusters_here, FAR1, K, K)
    shard_rows = lax.all_gather(cluster_rows, "leaf", axis=0, tiled=True)
    onehot = (cluster_source[:, :, None] == jnp.arange(shard_rows.shape[0])[None, None, :]).astype(
        jnp.float32
    )
    selected = jnp.einsum("ujn,nm->ujm", onehot, shard_rows, precision=highest_precision)
    selected = selected.reshape(clusters_here, FAR1, K, RHS)
    cluster_far = jnp.einsum("ujkl,ujlr->ukr", couplings, selected, precision=highest_precision)
    upper = cluster_transfer.reshape(clusters_here, K, K)
    projected = jnp.einsum("ukl,ulr->ukr", upper, cluster_coef, precision=highest_precision)
    projected_sum = projected.sum(axis=0).reshape(1, K * RHS)
    group_sum = lax.psum(projected_sum, "leaf")
    all_groups = lax.all_gather(group_sum, "group", axis=0, tiled=True)
    group_field = jnp.einsum(
        "hkl,hlr->kr",
        group_coupling.reshape(ngroups, K, K),
        all_groups.reshape(ngroups, K, RHS),
        precision=highest_precision,
    )
    cluster_field = cluster_far + jnp.einsum(
        "ulk,lr->ukr", upper, group_field, precision=highest_precision
    )
    spread_cluster = jnp.repeat(cluster_field, leaves_here // clusters_here, axis=0)
    leaf_field = leaf_far + jnp.einsum(
        "tlk,tlr->tkr", transfers, spread_cluster, precision=highest_precision
    )
    total = near_total + jnp.einsum("tka,tkr->tra", bases, leaf_field, precision=highest_precision)
    return total.transpose(1, 0, 2).reshape(RHS, leaves_here * LEAF)


def solution(mesh):
    in_specs = (
        P(None, ("group", "leaf")),
        P(("group", "leaf"), None, None),
        P(("group", "leaf"), None),
        P(("group", "leaf")),
        P(("group", "leaf"), None),
        P(("group", "leaf"), None),
        P(("group", "leaf"), None, None),
        P(("group", "leaf"), None),
        P(("group", "leaf"), None),
        P(("group", "leaf"), None, None),
        P(("group", "leaf"), None),
        P("group", None, None),
    )
    out_specs = P(None, ("group", "leaf"))
    return jax.shard_map(
        per_device, mesh=mesh, in_specs=in_specs, out_specs=out_specs, check_vma=False
    )
```

profile of v0, /device:TPU:0, one launch (start us, length us, event | category | flops | bytes accessed | tf_op | source)
XLA Modules:
  0.0 376.4 jit_solution(737260132806493097)
XLA Ops:
  0.0 1.4 collective-permute-start.1
  1.4 3.7 collective-permute-start
  5.2 1.1 reshape.73
  6.3 1.5 reshape.72
  7.8 2.0 fusion.15
  10.0 0.9 reshape.74
  10.9 1.3 collective-permute-start.3
  12.2 3.7 collective-permute-start.2
  16.1 0.9 copy.85
  17.0 1.7 bitcast_reduce_fusion
  18.9 60.3 %all-gather = f32[64,4,512]{2,1,0:T(4,128)S(1)} all-gather(f32[1,4,512]{2,1,0:T(4,128)S(1)} %reshape.105), channel_id=1, replica_groups=mesh['group'=4,'leaf'=64] {'leaf'}, dimensions={0}, use_global_device_ids=true | all-gather | bytes 532480 | tf_op jit(solution)/shard_map/all_gather | solution.py:81
  79.2 1.0 reshape.112
  80.2 1.4 fusion.18
  81.8 1.1 reshape.80
  83.3 126.7 %psum.7 = f32[1,512]{1,0:T(1,128)S(1)} all-reduce(f32[1,512]{1,0:T(1,128)S(1)} %reshape.82), channel_id=1, replica_groups=mesh['group'=4,'leaf'=64] {'leaf'}, use_global_device_ids=true, to_apply=%region_4.5 | all-reduce | flops 512 | bytes 4096 | tf_op jit(solution)/shard_map/psum | solution.py:91
  209.9 11.2 %all-gather.1 = f32[4,1,512]{2,1,0:T(1,128)S(1)} all-gather(f32[1,1,512]{2,1,0:T(1,128)S(1)} %bitcast.75), channel_id=1, replica_groups=mesh['group'=4,'leaf'=64] {'group'}, dimensions={0}, use_global_device_ids=true | all-gather | bytes 10240 | tf_op jit(solution)/shard_map/all_gather | solution.py:92
  221.4 1.0 convolution_bitcast_fusion.1
  222.9 3.8 %copy.82 = f32[64,8,1024]{0,2,1:T(8,128)} copy(f32[64,8,1024]{2,1,0:T(8,128)} %param.20) | data formatting | bytes 4194304 | tf_op args[6]
  226.7 9.1 %copy.83 = f32[64,8,32,32]{3,2,1,0:T(8,128)} copy(f32[64,8,32,32]{0,3,2,1:T(8,128)} %bitcast.67) | data formatting | bytes 4194304 | tf_op jit(solution)/shard_map/reshape | solution.py:72
  236.8 1.1 concatenate.13
  237.9 1.2 copy.80
  239.0 1.1 concatenate.12
  240.4 1.1 pad_maximum_fusion
  241.6 3.1 gather_fusion.1
  244.6 10.6 %fusion.10 = f32[64,16,32]{2,1,0:T(8,128)S(1)} fusion(f32[64,8,32,32]{3,2,1,0:T(8,128)} %copy.83, f32[64,8,16,32]{3,2,1,0:T(8,128)} %bitcast.68, pred[64,8]{1,0:T(8,128)(4,1)S(1)} %copy.76), kind=kOutput, calls=%fused_computation.19 | convolution fusion | flops 100925440 | bytes 3277312 | tf_op jit(solution)/shard_map/tjkl,rtjl->tkr/dot_general | solution.py:70
  255.3 1.8 convolution_add_fusion.1
  257.1 1.0 pad_maximum_fusion.1
  258.7 2.1 copy.74
  260.8 0.8 broadcast_in_dim.31
  261.6 111.1 %while.10 = (s32[]{:T(128)}, f32[64,16,64]{2,1,0:T(8,128)}, s32[]{:T(128)}, s32[64,8]{0,1:T(8,128)S(1)}, f32[192,16,64]{2,1,0:T(8,128)}, /*index=5*/f32[64,8,409...) while((s32[]{:T(128)}, f32[64,16,64]{2,1,0:T(8,128)}, s32[]{:T(128)}, ...), condition=%wide.region_2.0_spmd, body=%wide.region_1.2_spmd.sunk | while | flops 50529796 | bytes 8656923 | solution.py:65
  262.4 4.4 %constant_dynamic-slice_fusion.2 = f32[64,1,4096]{2,1,0:T(1,128)S(1)} fusion(f32[64,8,4096]{2,1,0:T(8,128)} %get-tuple-element.170, s32[]{:T(128)S(6)} %select_n.43), kind=kLoop, calls=%fused_computation.11.clone.1 | loop fusion | bytes 2097156 | tf_op jit(solution)/shard_map/while/body/jit(dynamic_index_in_dim)/dynamic_slice | solution.py:58
  267.5 0.8 reshape.124
  268.4 2.0 gather_fusion
  270.4 5.3 %fusion.45 = f32[64,16,64]{2,1,0:T(8,128)} fusion(f32[64,16,64]{2,1,0:T(8,128)} %get-tuple-element.156, f32[64,64,64]{2,1,0:T(8,128)S(1)} %reshape.124, f32[64,16,64]{2,1,0:T(8,128)S(1)} %gather_fusion, f32[64]{0:T(128)S(1)} %compare_convert_fusion.2, pred[64]{0:T(512)(128)(4,1)S(1)} %get-tuple-element.144), kind=kOutput, calls=%fused_computation.3.clone.1 | convolution fusion | flops 50528256 | bytes 1835328 | tf_op jit(solution)/shard_map/while/body/tab,trb->tra/dot_general | solution.py:62
  276.2 4.4 %constant_dynamic-slice_fusion.2 = f32[64,1,4096]{2,1,0:T(1,128)S(1)} fusion(f32[64,8,4096]{2,1,0:T(8,128)} %get-tuple-element.170, s32[]{:T(128)S(6)} %select_n.43), kind=kLoop, calls=%fused_computation.11.clone.1 | loop fusion | bytes 2097156 | tf_op jit(solution)/shard_map/while/body/jit(dynamic_index_in_dim)/dynamic_slice | solution.py:58
  281.3 0.8 reshape.124
  282.2 2.0 gather_fusion
  284.2 5.3 %fusion.45 = f32[64,16,64]{2,1,0:T(8,128)} fusion(f32[64,16,64]{2,1,0:T(8,128)} %get-tuple-element.156, f32[64,64,64]{2,1,0:T(8,128)S(1)} %reshape.124, f32[64,16,64]{2,1,0:T(8,128)S(1)} %gather_fusion, f32[64]{0:T(128)S(1)} %compare_convert_fusion.2, pred[64]{0:T(512)(128)(4,1)S(1)} %get-tuple-element.144), kind=kOutput, calls=%fused_computation.3.clone.1 | convolution fusion | flops 50528256 | bytes 1835328 | tf_op jit(solution)/shard_map/while/body/tab,trb->tra/dot_general | solution.py:62
  290.0 4.4 %constant_dynamic-slice_fusion.2 = f32[64,1,4096]{2,1,0:T(1,128)S(1)} fusion(f32[64,8,4096]{2,1,0:T(8,128)} %get-tuple-element.170, s32[]{:T(128)S(6)} %select_n.43), kind=kLoop, calls=%fused_computation.11.clone.1 | loop fusion | bytes 2097156 | tf_op jit(solution)/shard_map/while/body/jit(dynamic_index_in_dim)/dynamic_slice | solution.py:58
  295.1 0.8 reshape.124
  295.9 2.0 gather_fusion
  298.0 5.3 %fusion.45 = f32[64,16,64]{2,1,0:T(8,128)} fusion(f32[64,16,64]{2,1,0:T(8,128)} %get-tuple-element.156, f32[64,64,64]{2,1,0:T(8,128)S(1)} %reshape.124, f32[64,16,64]{2,1,0:T(8,128)S(1)} %gather_fusion, f32[64]{0:T(128)S(1)} %compare_convert_fusion.2, pred[64]{0:T(512)(128)(4,1)S(1)} %get-tuple-element.144), kind=kOutput, calls=%fused_computation.3.clone.1 | convolution fusion | flops 50528256 | bytes 1835328 | tf_op jit(solution)/shard_map/while/body/tab,trb->tra/dot_general | solution.py:62
  303.8 4.4 %constant_dynamic-slice_fusion.2 = f32[64,1,4096]{2,1,0:T(1,128)S(1)} fusion(f32[64,8,4096]{2,1,0:T(8,128)} %get-tuple-element.170, s32[]{:T(128)S(6)} %select_n.43), kind=kLoop, calls=%fused_computation.11.clone.1 | loop fusion | bytes 2097156 | tf_op jit(solution)/shard_map/while/body/jit(dynamic_index_in_dim)/dynamic_slice | solution.py:58
  308.9 0.8 reshape.124
  309.7 2.0 gather_fusion
  311.8 5.3 %fusion.45 = f32[64,16,64]{2,1,0:T(8,128)} fusion(f32[64,16,64]{2,1,0:T(8,128)} %get-tuple-element.156, f32[64,64,64]{2,1,0:T(8,128)S(1)} %reshape.124, f32[64,16,64]{2,1,0:T(8,128)S(1)} %gather_fusion, f32[64]{0:T(128)S(1)} %compare_convert_fusion.2, pred[64]{0:T(512)(128)(4,1)S(1)} %get-tuple-element.144), kind=kOutput, calls=%fused_computation.3.clone.1 | convolution fusion | flops 50528256 | bytes 1835328 | tf_op jit(solution)/shard_map/while/body/tab,trb->tra/dot_general | solution.py:62
  317.6 4.4 %constant_dynamic-slice_fusion.2 = f32[64,1,4096]{2,1,0:T(1,128)S(1)} fusion(f32[64,8,4096]{2,1,0:T(8,128)} %get-tuple-element.170, s32[]{:T(128)S(6)} %select_n.43), kind=kLoop, calls=%fused_computation.11.clone.1 | loop fusion | bytes 2097156 | tf_op jit(solution)/shard_map/while/body/jit(dynamic_index_in_dim)/dynamic_slice | solution.py:58
  322.7 0.8 reshape.124
  323.5 2.0 gather_fusion
  325.5 5.3 %fusion.45 = f32[64,16,64]{2,1,0:T(8,128)} fusion(f32[64,16,64]{2,1,0:T(8,128)} %get-tuple-element.156, f32[64,64,64]{2,1,0:T(8,128)S(1)} %reshape.124, f32[64,16,64]{2,1,0:T(8,128)S(1)} %gather_fusion, f32[64]{0:T(128)S(1)} %compare_convert_fusion.2, pred[64]{0:T(512)(128)(4,1)S(1)} %get-tuple-element.144), kind=kOutput, calls=%fused_computation.3.clone.1 | convolution fusion | flops 50528256 | bytes 1835328 | tf_op jit(solution)/shard_map/while/body/tab,trb->tra/dot_general | solution.py:62
  331.4 4.4 %constant_dynamic-slice_fusion.2 = f32[64,1,4096]{2,1,0:T(1,128)S(1)} fusion(f32[64,8,4096]{2,1,0:T(8,128)} %get-tuple-element.170, s32[]{:T(128)S(6)} %select_n.43), kind=kLoop, calls=%fused_computation.11.clone.1 | loop fusion | bytes 2097156 | tf_op jit(solution)/shard_map/while/body/jit(dynamic_index_in_dim)/dynamic_slice | solution.py:58
  336.4 0.8 reshape.124
  337.3 2.0 gather_fusion
  339.3 5.3 %fusion.45 = f32[64,16,64]{2,1,0:T(8,128)} fusion(f32[64,16,64]{2,1,0:T(8,128)} %get-tuple-element.156, f32[64,64,64]{2,1,0:T(8,128)S(1)} %reshape.124, f32[64,16,64]{2,1,0:T(8,128)S(1)} %gather_fusion, f32[64]{0:T(128)S(1)} %compare_convert_fusion.2, pred[64]{0:T(512)(128)(4,1)S(1)} %get-tuple-element.144), kind=kOutput, calls=%fused_computation.3.clone.1 | convolution fusion | flops 50528256 | bytes 1835328 | tf_op jit(solution)/shard_map/while/body/tab,trb->tra/dot_general | solution.py:62
  345.2 4.4 %constant_dynamic-slice_fusion.2 = f32[64,1,4096]{2,1,0:T(1,128)S(1)} fusion(f32[64,8,4096]{2,1,0:T(8,128)} %get-tuple-element.170, s32[]{:T(128)S(6)} %select_n.43), kind=kLoop, calls=%fused_computation.11.clone.1 | loop fusion | bytes 2097156 | tf_op jit(solution)/shard_map/while/body/jit(dynamic_index_in_dim)/dynamic_slice | solution.py:58
  350.2 0.8 reshape.124
  351.1 2.0 gather_fusion
  353.1 5.3 %fusion.45 = f32[64,16,64]{2,1,0:T(8,128)} fusion(f32[64,16,64]{2,1,0:T(8,128)} %get-tuple-element.156, f32[64,64,64]{2,1,0:T(8,128)S(1)} %reshape.124, f32[64,16,64]{2,1,0:T(8,128)S(1)} %gather_fusion, f32[64]{0:T(128)S(1)} %compare_convert_fusion.2, pred[64]{0:T(512)(128)(4,1)S(1)} %get-tuple-element.144), kind=kOutput, calls=%fused_computation.3.clone.1 | convolution fusion | flops 50528256 | bytes 1835328 | tf_op jit(solution)/shard_map/while/body/tab,trb->tra/dot_general | solution.py:62
  359.0 4.4 %constant_dynamic-slice_fusion.2 = f32[64,1,4096]{2,1,0:T(1,128)S(1)} fusion(f32[64,8,4096]{2,1,0:T(8,128)} %get-tuple-element.170, s32[]{:T(128)S(6)} %select_n.43), kind=kLoop, calls=%fused_computation.11.clone.1 | loop fusion | bytes 2097156 | tf_op jit(solution)/shard_map/while/body/jit(dynamic_index_in_dim)/dynamic_slice | solution.py:58
  364.0 0.8 reshape.124
  364.9 2.0 gather_fusion
  366.9 5.3 %fusion.45 = f32[64,16,64]{2,1,0:T(8,128)} fusion(f32[64,16,64]{2,1,0:T(8,128)} %get-tuple-element.156, f32[64,64,64]{2,1,0:T(8,128)S(1)} %reshape.124, f32[64,16,64]{2,1,0:T(8,128)S(1)} %gather_fusion, f32[64]{0:T(128)S(1)} %compare_convert_fusion.2, pred[64]{0:T(512)(128)(4,1)S(1)} %get-tuple-element.144), kind=kOutput, calls=%fused_computation.3.clone.1 | convolution fusion | flops 50528256 | bytes 1835328 | tf_op jit(solution)/shard_map/while/body/tab,trb->tra/dot_general | solution.py:62
  372.7 2.6 fusion.13
  375.5 0.9 reshape.86
  (79 shorter events, 9.0 us)
Async XLA Ops:
  0.0 15.8 %copy-start.2 = (f32[64,1024]{1,0:T(8,128)S(1)}, f32[64,1024]{1,0:T(8,128)}, u32[]{:S(2)}) copy-start(f32[64,1024]{1,0:T(8,128)} %param.21) | copy-start | bytes 786436
  0.0 257.1 %collective-permute-start.1 = (f32[16,4096]{1,0:T(8,128)}, f32[16,4096]{1,0:T(8,128)S(1)}, u32[]{:S(2)}, u32[]{:S(2)}) collective-permute-start(f32[16,4096]{1,0:T(8,128)} %param.14), channel_id=1, source_target_pairs={{1,0},{2,1},{3,2},{4,3},{5,4},{6,5},{7,6},{8,7},{9,8},{10,9},{11,1... | collective-permute-start | bytes 786440 | tf_op jit(solution)/shard_map/ppermute | solution.py:22
  1.4 255.7 %collective-permute-start = (f32[16,4096]{1,0:T(8,128)}, f32[16,4096]{1,0:T(8,128)}, u32[]{:S(2)}, u32[]{:S(2)}) collective-permute-start(f32[16,4096]{1,0:T(8,128)} %param.14), channel_id=1, source_target_pairs={{0,1},{1,2},{2,3},{3,4},{4,5},{5,6},{6,7},{7,8},{8,9},{9,10},{10,1... | collective-permute-start | bytes 786440 | tf_op jit(solution)/shard_map/ppermute | solution.py:21
  7.8 71.4 %copy-start = (f32[64,32,64]{2,1,0:T(8,128)}, f32[64,32,64]{2,1,0:T(8,128)S(1)}, u32[]{:S(2)}) copy-start(f32[64,32,64]{2,1,0:T(8,128)S(1)} %reshape.72) | copy-start | bytes 1572868
  9.7 70.4 %copy-start.7 = (s32[4,8]{1,0:T(4,128)S(1)}, s32[4,8]{1,0:T(4,128)}, u32[]{:S(2)}) copy-start(s32[4,8]{1,0:T(4,128)} %param.22) | copy-start | bytes 388
  9.9 72.9 %copy-start.3 = (f32[4,1024]{1,0:T(4,128)S(1)}, f32[4,1024]{1,0:T(4,128)}, u32[]{:S(2)}) copy-start(f32[4,1024]{1,0:T(4,128)} %param.24) | copy-start | bytes 49156
  9.9 211.4 %copy-start.4 = (f32[1,4,1024]{2,1,0:T(4,128)S(1)}, f32[1,4,1024]{2,1,0:T(4,128)}, u32[]{:S(2)}) copy-start(f32[1,4,1024]{2,1,0:T(4,128)} %param.25) | copy-start | bytes 49156
  10.0 211.4 %copy-start.5 = (s32[64,8]{0,1:T(8,128)S(1)}, s32[64,8]{0,1:T(8,128)}, u32[]{:S(2)}) copy-start(s32[64,8]{0,1:T(8,128)} %param.19) | copy-start | bytes 6148
  10.9 225.9 %collective-permute-start.3 = (f32[16,2048]{1,0:T(8,128)}, f32[16,2048]{1,0:T(8,128)}, u32[]{:S(2)}, u32[]{:S(2)}) collective-permute-start(f32[16,2048]{1,0:T(8,128)} %reshape.74), channel_id=1, source_target_pairs={{1,0},{2,1},{3,2},{4,3},{5,4},{6,5},{7,6},{8,7},{9,8},{10,9},{11,1... | collective-permute-start | bytes 393224 | tf_op jit(solution)/shard_map/ppermute | solution.py:22
  12.2 226.9 %collective-permute-start.2 = (f32[16,2048]{1,0:T(8,128)}, f32[16,2048]{1,0:T(8,128)}, u32[]{:S(2)}, u32[]{:S(2)}) collective-permute-start(f32[16,2048]{1,0:T(8,128)} %reshape.74), channel_id=1, source_target_pairs={{0,1},{1,2},{2,3},{3,4},{4,5},{5,6},{6,7},{7,8},{8,9},{9,10},{10,1... | collective-permute-start | bytes 393224 | tf_op jit(solution)/shard_map/ppermute | solution.py:21
  16.0 206.8 %copy-start.6 = (s32[64,8]{0,1:T(8,128)S(1)}, s32[64,8]{0,1:T(8,128)}, u32[]{:S(2)}) copy-start(s32[64,8]{0,1:T(8,128)} %param.16) | copy-start | bytes 6148
  226.7 9.4 %copy-start.8 = (s32[64]{0:T(128)S(1)}, s32[64]{0:T(128)}, u32[]{:S(2)}) copy-start(s32[64]{0:T(128)} %param.17) | copy-start | bytes 772
  244.6 12.5 %copy-start.1 = (f32[16,4096]{1,0:T(8,128)S(1)}, f32[16,4096]{1,0:T(8,128)}, u32[]{:S(2)}) copy-start(f32[16,4096]{1,0:T(8,128)} %param.14) | copy-start | bytes 786436
where the time goes:
time: 378 us; the launch traced here: 376 us
  blocking collectives  198 us (52%)
  local copies, waits for them, and re-layouts  95.3 us (25%)
  matrix products  63.6 us (17%)
  starting transfers between devices  10.1 us (3%)
  loops' own time  5.86 us (2%)
    psum x1, blocking collectives, per_device(): group_sum = lax.psum(projected_sum, 'leaf')  127 us
    all_gather x1, blocking collectives, per_device(): shard_rows = lax.all_gather(cluster_rows, 'leaf', axis=0, tiled=True)  60.3 us
    dot_general x8, matrix products, near_step(): term = jnp.einsum('tab,trb->tra', slab, picked, precision=highest_precision)  42 us
    dynamic_slice x16, local copies, waits for them, and re-layouts, near_step(): lax.dynamic_index_in_dim(near_blocks, slot_index, axis=1, keepdims=False)  40.3 us
    gather x8, local copies, waits for them, and re-layouts, near_step(): picked = jnp.take(point_blocks, near_local[:, slot_index], axis=0)  16 us
    all_gather x1, blocking collectives, per_device(): all_groups = lax.all_gather(group_sum, 'group', axis=0, tiled=True)  11.2 us
    dot_general x1, matrix products, per_device(): jnp.einsum('tjkl,rtjl->tkr', leaf_coupling.reshape(leaves_here, FAR0, K,...  10.6 us
    reshape x1, local copies, waits for them, and re-layouts, per_device(): leaf_coupling.reshape(leaves_here, FAR0, K, K)  9.12 us
  transfers between devices with their start and end apart: 4, of which 0 were waited for; matrix products, arithmetic and copies ran while one was open for 13% of the time, Pallas kernels for 0%

commit v1 on v0

--- a/solution.py
+++ b/solution.py
@@ -89,7 +89,14 @@
     projected = jnp.einsum("ukl,ulr->ukr", upper, cluster_coef, precision=highest_precision)
     projected_sum = projected.sum(axis=0).reshape(1, K * RHS)
     group_sum = lax.psum(projected_sum, "leaf")
-    all_groups = lax.all_gather(group_sum, "group", axis=0, tiled=True)
+    ring = [group_sum]
+    for hop in range(3):
+        ring.append(lax.ppermute(ring[-1], "group", [(dev, (dev + 1) % 4) for dev in range(4)]))
+    all_groups = jnp.roll(
+        jnp.concatenate(ring[::-1], axis=0),
+        (lax.axis_index("group") + 1) * ring[0].shape[0],
+        axis=0,
+    )
     group_field = jnp.einsum(
         "hkl,hlr->kr",
         group_coupling.reshape(ngroups, K, K),

time: 378 us -> 378 us (level)
  blocking collectives: 198 us -> 191 us
    psum x1, blocking collectives: 127 us -> 140 us  [per_device(): group_sum = lax.psum(projected_sum, 'leaf')]
    all_gather x1 -> x0, blocking collectives: 11.2 us -> none  [per_device(): all_groups = lax.all_gather(group_sum, 'group', axis=0, tiled=True)]
    all_gather x1, blocking collectives: 60.3 us -> 51.8 us  [per_device(): shard_rows = lax.all_gather(cluster_rows, 'leaf', axis=0, tiled=True)]
  transfers between devices with their start and end apart: 4 -> 7, of which waited for: 0 -> 1; matrix products, arithmetic and copies ran while one was open for 13% -> 13% of each run, Pallas kernels for 0% -> 0%
where the time goes in v1:
time: 378 us; the launch traced here: 376 us
  blocking collectives  191 us (51%)
  local copies, waits for them, and re-layouts  95.6 us (25%)
  matrix products  62.7 us (17%)
  starting transfers between devices  13.5 us (4%)
  loops' own time  7.01 us (2%)
    psum x1, blocking collectives, per_device(): group_sum = lax.psum(projected_sum, 'leaf')  140 us
    all_gather x1, blocking collectives, per_device(): shard_rows = lax.all_gather(cluster_rows, 'leaf', axis=0, tiled=True)  51.8 us
    dot_general x8, matrix products, near_step(): term = jnp.einsum('tab,trb->tra', slab, picked, precision=highest_precision)  42.1 us
    dynamic_slice x16, local copies, waits for them, and re-layouts, near_step(): lax.dynamic_index_in_dim(near_blocks, slot_index, axis=1, keepdims=False)  40.3 us
    gather x8, local copies, waits for them, and re-layouts, near_step(): picked = jnp.take(point_blocks, near_local[:, slot_index], axis=0)  16 us
    dot_general x1, matrix products, per_device(): jnp.einsum('tjkl,rtjl->tkr', leaf_coupling.reshape(leaves_here, FAR0, K,...  10.6 us
    reshape x1, local copies, waits for them, and re-layouts, per_device(): leaf_coupling.reshape(leaves_here, FAR0, K, K)  9.18 us
  transfers between devices with their start and end apart: 7, of which 1 were waited for; matrix products, arithmetic and copies ran while one was open for 13% of the time, Pallas kernels for 0%

profile of v1, /device:TPU:0, one launch (start us, length us, event | category | flops | bytes accessed | tf_op | source)
XLA Modules:
  0.0 375.9 jit_solution(11243140613233326289)
XLA Ops:
  0.0 1.4 collective-permute-start.1
  1.4 3.7 collective-permute-start
  5.2 1.1 reshape.73
  6.3 1.5 reshape.72
  7.8 2.0 fusion.15
  10.0 0.9 reshape.74
  10.9 1.3 collective-permute-start.3
  12.2 3.7 collective-permute-start.2
  16.1 0.9 copy.85
  17.0 1.7 bitcast_reduce_fusion
  19.2 139.6 %psum.7 = f32[1,512]{1,0:T(1,128)S(1)} all-reduce(f32[1,512]{1,0:T(1,128)S(1)} %reshape.82), channel_id=1, replica_groups=mesh['group'=4,'leaf'=64] {'leaf'}, use_global_device_ids=true, to_apply=%region_4.5 | all-reduce | flops 512 | bytes 4096 | tf_op jit(solution)/shard_map/psum | solution.py:91
  158.8 1.5 collective-permute-start.4
  160.5 51.8 %all-gather = f32[64,4,512]{2,1,0:T(4,128)} all-gather(f32[1,4,512]{2,1,0:T(4,128)S(1)} %reshape.105), channel_id=1, replica_groups=mesh['group'=4,'leaf'=64] {'leaf'}, dimensions={0}, use_global_device_ids=true | all-gather | bytes 532480 | tf_op jit(solution)/shard_map/all_gather | solution.py:81
  212.4 1.2 reshape.109
  214.2 1.1 reshape.80
  215.3 1.6 collective-permute-start.5
  216.9 1.0 convolution_bitcast_fusion.1
  218.0 2.1 collective-permute-done.5
  220.4 3.8 %copy.82 = f32[64,8,1024]{0,2,1:T(8,128)} copy(f32[64,8,1024]{2,1,0:T(8,128)} %param.20) | data formatting | bytes 4194304 | tf_op args[6]
  224.3 9.2 %copy.83 = f32[64,8,32,32]{3,2,1,0:T(8,128)} copy(f32[64,8,32,32]{0,3,2,1:T(8,128)} %bitcast.66) | data formatting | bytes 4194304 | tf_op jit(solution)/shard_map/reshape | solution.py:72
  235.0 1.1 concatenate.19
  236.1 1.1 copy.80
  237.2 1.1 concatenate.18
  238.6 1.1 pad_maximum_fusion
  239.8 3.1 gather_fusion.1
  242.9 10.6 %fusion.10 = f32[64,16,32]{2,1,0:T(8,128)S(1)} fusion(f32[64,8,32,32]{3,2,1,0:T(8,128)} %copy.83, f32[64,8,16,32]{3,2,1,0:T(8,128)} %bitcast.67, pred[64,8]{1,0:T(8,128)(4,1)S(1)} %copy.76), kind=kOutput, calls=%fused_computation.19 | convolution fusion | flops 100925440 | bytes 3277312 | tf_op jit(solution)/shard_map/tjkl,rtjl->tkr/dot_general | solution.py:70
  253.5 1.8 convolution_add_fusion.1
  255.4 1.0 pad_maximum_fusion.1
  257.0 2.1 copy.74
  259.1 0.8 broadcast_in_dim.31
  259.9 112.3 %while.10 = (s32[]{:T(128)}, f32[64,16,64]{2,1,0:T(8,128)}, s32[]{:T(128)}, s32[64,8]{0,1:T(8,128)S(1)}, f32[192,16,64]{2,1,0:T(8,128)}, /*index=5*/f32[64,8,409...) while((s32[]{:T(128)}, f32[64,16,64]{2,1,0:T(8,128)}, s32[]{:T(128)}, ...), condition=%wide.region_2.0_spmd, body=%wide.region_1.2_spmd.sunk | while | flops 50529796 | bytes 8656923 | solution.py:65
  260.8 4.4 %constant_dynamic-slice_fusion.3 = f32[64,1,4096]{2,1,0:T(1,128)S(1)} fusion(f32[64,8,4096]{2,1,0:T(8,128)} %get-tuple-element.170, s32[]{:T(128)S(6)} %select_n.58), kind=kLoop, calls=%fused_computation.11.clone.1 | loop fusion | bytes 2097156 | tf_op jit(solution)/shard_map/while/body/jit(dynamic_index_in_dim)/dynamic_slice | solution.py:58
  265.9 0.8 reshape.120
  266.8 2.0 gather_fusion
  268.8 5.3 %fusion.45 = f32[64,16,64]{2,1,0:T(8,128)} fusion(f32[64,16,64]{2,1,0:T(8,128)} %get-tuple-element.156, f32[64,64,64]{2,1,0:T(8,128)S(1)} %reshape.120, f32[64,16,64]{2,1,0:T(8,128)S(1)} %gather_fusion, f32[64]{0:T(128)S(1)} %compare_convert_fusion.2, pred[64]{0:T(512)(128)(4,1)S(1)} %get-tuple-element.144), kind=kOutput, calls=%fused_computation.3.clone.1 | convolution fusion | flops 50528256 | bytes 1835328 | tf_op jit(solution)/shard_map/while/body/tab,trb->tra/dot_general | solution.py:62
  274.8 4.4 %constant_dynamic-slice_fusion.3 = f32[64,1,4096]{2,1,0:T(1,128)S(1)} fusion(f32[64,8,4096]{2,1,0:T(8,128)} %get-tuple-element.170, s32[]{:T(128)S(6)} %select_n.58), kind=kLoop, calls=%fused_computation.11.clone.1 | loop fusion | bytes 2097156 | tf_op jit(solution)/shard_map/while/body/jit(dynamic_index_in_dim)/dynamic_slice | solution.py:58
  279.8 0.8 reshape.120
  280.7 2.0 gather_fusion
  282.7 5.3 %fusion.45 = f32[64,16,64]{2,1,0:T(8,128)} fusion(f32[64,16,64]{2,1,0:T(8,128)} %get-tuple-element.156, f32[64,64,64]{2,1,0:T(8,128)S(1)} %reshape.120, f32[64,16,64]{2,1,0:T(8,128)S(1)} %gather_fusion, f32[64]{0:T(128)S(1)} %compare_convert_fusion.2, pred[64]{0:T(512)(128)(4,1)S(1)} %get-tuple-element.144), kind=kOutput, calls=%fused_computation.3.clone.1 | convolution fusion | flops 50528256 | bytes 1835328 | tf_op jit(solution)/shard_map/while/body/tab,trb->tra/dot_general | solution.py:62
  288.7 4.4 %constant_dynamic-slice_fusion.3 = f32[64,1,4096]{2,1,0:T(1,128)S(1)} fusion(f32[64,8,4096]{2,1,0:T(8,128)} %get-tuple-element.170, s32[]{:T(128)S(6)} %select_n.58), kind=kLoop, calls=%fused_computation.11.clone.1 | loop fusion | bytes 2097156 | tf_op jit(solution)/shard_map/while/body/jit(dynamic_index_in_dim)/dynamic_slice | solution.py:58
  293.7 0.8 reshape.120
  294.6 2.0 gather_fusion
  296.6 5.3 %fusion.45 = f32[64,16,64]{2,1,0:T(8,128)} fusion(f32[64,16,64]{2,1,0:T(8,128)} %get-tuple-element.156, f32[64,64,64]{2,1,0:T(8,128)S(1)} %reshape.120, f32[64,16,64]{2,1,0:T(8,128)S(1)} %gather_fusion, f32[64]{0:T(128)S(1)} %compare_convert_fusion.2, pred[64]{0:T(512)(128)(4,1)S(1)} %get-tuple-element.144), kind=kOutput, calls=%fused_computation.3.clone.1 | convolution fusion | flops 50528256 | bytes 1835328 | tf_op jit(solution)/shard_map/while/body/tab,trb->tra/dot_general | solution.py:62
  302.6 4.4 %constant_dynamic-slice_fusion.3 = f32[64,1,4096]{2,1,0:T(1,128)S(1)} fusion(f32[64,8,4096]{2,1,0:T(8,128)} %get-tuple-element.170, s32[]{:T(128)S(6)} %select_n.58), kind=kLoop, calls=%fused_computation.11.clone.1 | loop fusion | bytes 2097156 | tf_op jit(solution)/shard_map/while/body/jit(dynamic_index_in_dim)/dynamic_slice | solution.py:58
  307.7 0.8 reshape.120
  308.6 2.0 gather_fusion
  310.6 5.3 %fusion.45 = f32[64,16,64]{2,1,0:T(8,128)} fusion(f32[64,16,64]{2,1,0:T(8,128)} %get-tuple-element.156, f32[64,64,64]{2,1,0:T(8,128)S(1)} %reshape.120, f32[64,16,64]{2,1,0:T(8,128)S(1)} %gather_fusion, f32[64]{0:T(128)S(1)} %compare_convert_fusion.2, pred[64]{0:T(512)(128)(4,1)S(1)} %get-tuple-element.144), kind=kOutput, calls=%fused_computation.3.clone.1 | convolution fusion | flops 50528256 | bytes 1835328 | tf_op jit(solution)/shard_map/while/body/tab,trb->tra/dot_general | solution.py:62
  316.6 4.4 %constant_dynamic-slice_fusion.3 = f32[64,1,4096]{2,1,0:T(1,128)S(1)} fusion(f32[64,8,4096]{2,1,0:T(8,128)} %get-tuple-element.170, s32[]{:T(128)S(6)} %select_n.58), kind=kLoop, calls=%fused_computation.11.clone.1 | loop fusion | bytes 2097156 | tf_op jit(solution)/shard_map/while/body/jit(dynamic_index_in_dim)/dynamic_slice | solution.py:58
  321.6 0.8 reshape.120
  322.5 2.0 gather_fusion
  324.5 5.3 %fusion.45 = f32[64,16,64]{2,1,0:T(8,128)} fusion(f32[64,16,64]{2,1,0:T(8,128)} %get-tuple-element.156, f32[64,64,64]{2,1,0:T(8,128)S(1)} %reshape.120, f32[64,16,64]{2,1,0:T(8,128)S(1)} %gather_fusion, f32[64]{0:T(128)S(1)} %compare_convert_fusion.2, pred[64]{0:T(512)(128)(4,1)S(1)} %get-tuple-element.144), kind=kOutput, calls=%fused_computation.3.clone.1 | convolution fusion | flops 50528256 | bytes 1835328 | tf_op jit(solution)/shard_map/while/body/tab,trb->tra/dot_general | solution.py:62
  330.5 4.4 %constant_dynamic-slice_fusion.3 = f32[64,1,4096]{2,1,0:T(1,128)S(1)} fusion(f32[64,8,4096]{2,1,0:T(8,128)} %get-tuple-element.170, s32[]{:T(128)S(6)} %select_n.58), kind=kLoop, calls=%fused_computation.11.clone.1 | loop fusion | bytes 2097156 | tf_op jit(solution)/shard_map/while/body/jit(dynamic_index_in_dim)/dynamic_slice | solution.py:58
  335.5 0.8 reshape.120
  336.4 2.0 gather_fusion
  338.4 5.3 %fusion.45 = f32[64,16,64]{2,1,0:T(8,128)} fusion(f32[64,16,64]{2,1,0:T(8,128)} %get-tuple-element.156, f32[64,64,64]{2,1,0:T(8,128)S(1)} %reshape.120, f32[64,16,64]{2,1,0:T(8,128)S(1)} %gather_fusion, f32[64]{0:T(128)S(1)} %compare_convert_fusion.2, pred[64]{0:T(512)(128)(4,1)S(1)} %get-tuple-element.144), kind=kOutput, calls=%fused_computation.3.clone.1 | convolution fusion | flops 50528256 | bytes 1835328 | tf_op jit(solution)/shard_map/while/body/tab,trb->tra/dot_general | solution.py:62
  344.4 4.4 %constant_dynamic-slice_fusion.3 = f32[64,1,4096]{2,1,0:T(1,128)S(1)} fusion(f32[64,8,4096]{2,1,0:T(8,128)} %get-tuple-element.170, s32[]{:T(128)S(6)} %select_n.58), kind=kLoop, calls=%fused_computation.11.clone.1 | loop fusion | bytes 2097156 | tf_op jit(solution)/shard_map/while/body/jit(dynamic_index_in_dim)/dynamic_slice | solution.py:58
  350.3 2.0 gather_fusion
  352.4 5.3 %fusion.45 = f32[64,16,64]{2,1,0:T(8,128)} fusion(f32[64,16,64]{2,1,0:T(8,128)} %get-tuple-element.156, f32[64,64,64]{2,1,0:T(8,128)S(1)} %reshape.120, f32[64,16,64]{2,1,0:T(8,128)S(1)} %gather_fusion, f32[64]{0:T(128)S(1)} %compare_convert_fusion.2, pred[64]{0:T(512)(128)(4,1)S(1)} %get-tuple-element.144), kind=kOutput, calls=%fused_computation.3.clone.1 | convolution fusion | flops 50528256 | bytes 1835328 | tf_op jit(solution)/shard_map/while/body/tab,trb->tra/dot_general | solution.py:62
  358.3 4.4 %constant_dynamic-slice_fusion.3 = f32[64,1,4096]{2,1,0:T(1,128)S(1)} fusion(f32[64,8,4096]{2,1,0:T(8,128)} %get-tuple-element.170, s32[]{:T(128)S(6)} %select_n.58), kind=kLoop, calls=%fused_computation.11.clone.1 | loop fusion | bytes 2097156 | tf_op jit(solution)/shard_map/while/body/jit(dynamic_index_in_dim)/dynamic_slice | solution.py:58
  363.4 0.8 reshape.120
  364.3 2.0 gather_fusion
  366.3 5.3 %fusion.45 = f32[64,16,64]{2,1,0:T(8,128)} fusion(f32[64,16,64]{2,1,0:T(8,128)} %get-tuple-element.156, f32[64,64,64]{2,1,0:T(8,128)S(1)} %reshape.120, f32[64,16,64]{2,1,0:T(8,128)S(1)} %gather_fusion, f32[64]{0:T(128)S(1)} %compare_convert_fusion.2, pred[64]{0:T(512)(128)(4,1)S(1)} %get-tuple-element.144), kind=kOutput, calls=%fused_computation.3.clone.1 | convolution fusion | flops 50528256 | bytes 1835328 | tf_op jit(solution)/shard_map/while/body/tab,trb->tra/dot_general | solution.py:62
  372.3 2.6 fusion.13
  375.0 0.9 reshape.86
  (85 shorter events, 10.5 us)
Async XLA Ops:
  0.0 15.9 %copy-start.2 = (f32[64,1024]{1,0:T(8,128)S(1)}, f32[64,1024]{1,0:T(8,128)}, u32[]{:S(2)}) copy-start(f32[64,1024]{1,0:T(8,128)} %param.21) | copy-start | bytes 786436
  0.0 255.3 %collective-permute-start.1 = (f32[16,4096]{1,0:T(8,128)}, f32[16,4096]{1,0:T(8,128)S(1)}, u32[]{:S(2)}, u32[]{:S(2)}) collective-permute-start(f32[16,4096]{1,0:T(8,128)} %param.14), channel_id=1, source_target_pairs={{1,0},{2,1},{3,2},{4,3},{5,4},{6,5},{7,6},{8,7},{9,8},{10,9},{11,1... | collective-permute-start | bytes 786440 | tf_op jit(solution)/shard_map/ppermute | solution.py:22
  1.4 253.9 %collective-permute-start = (f32[16,4096]{1,0:T(8,128)}, f32[16,4096]{1,0:T(8,128)}, u32[]{:S(2)}, u32[]{:S(2)}) collective-permute-start(f32[16,4096]{1,0:T(8,128)} %param.14), channel_id=1, source_target_pairs={{0,1},{1,2},{2,3},{3,4},{4,5},{5,6},{6,7},{7,8},{8,9},{9,10},{10,1... | collective-permute-start | bytes 786440 | tf_op jit(solution)/shard_map/ppermute | solution.py:21
  7.8 204.6 %copy-start = (f32[64,32,64]{2,1,0:T(8,128)}, f32[64,32,64]{2,1,0:T(8,128)S(1)}, u32[]{:S(2)}) copy-start(f32[64,32,64]{2,1,0:T(8,128)S(1)} %reshape.72) | copy-start | bytes 1572868
  7.8 10.9 %copy-start.3 = (f32[4,1024]{1,0:T(4,128)S(1)}, f32[4,1024]{1,0:T(4,128)}, u32[]{:S(2)}) copy-start(f32[4,1024]{1,0:T(4,128)} %param.24) | copy-start | bytes 49156
  9.8 203.8 %copy-start.5 = (s32[64,8]{0,1:T(8,128)S(1)}, s32[64,8]{0,1:T(8,128)}, u32[]{:S(2)}) copy-start(s32[64,8]{0,1:T(8,128)} %param.19) | copy-start | bytes 6148
  9.8 203.8 %copy-start.7 = (s32[4,8]{1,0:T(4,128)S(1)}, s32[4,8]{1,0:T(4,128)}, u32[]{:S(2)}) copy-start(s32[4,8]{1,0:T(4,128)} %param.22) | copy-start | bytes 388
  9.8 204.2 %copy-start.6 = (s32[64,8]{0,1:T(8,128)S(1)}, s32[64,8]{0,1:T(8,128)}, u32[]{:S(2)}) copy-start(s32[64,8]{0,1:T(8,128)} %param.16) | copy-start | bytes 6148
  10.9 224.1 %collective-permute-start.3 = (f32[16,2048]{1,0:T(8,128)}, f32[16,2048]{1,0:T(8,128)}, u32[]{:S(2)}, u32[]{:S(2)}) collective-permute-start(f32[16,2048]{1,0:T(8,128)} %reshape.74), channel_id=1, source_target_pairs={{1,0},{2,1},{3,2},{4,3},{5,4},{6,5},{7,6},{8,7},{9,8},{10,9},{11,1... | collective-permute-start | bytes 393224 | tf_op jit(solution)/shard_map/ppermute | solution.py:22
  12.2 225.1 %collective-permute-start.2 = (f32[16,2048]{1,0:T(8,128)}, f32[16,2048]{1,0:T(8,128)}, u32[]{:S(2)}, u32[]{:S(2)}) collective-permute-start(f32[16,2048]{1,0:T(8,128)} %reshape.74), channel_id=1, source_target_pairs={{0,1},{1,2},{2,3},{3,4},{4,5},{5,6},{6,7},{7,8},{8,9},{9,10},{10,1... | collective-permute-start | bytes 393224 | tf_op jit(solution)/shard_map/ppermute | solution.py:21
  158.8 56.5 %collective-permute-start.4 = (f32[1,512]{1,0:T(1,128)S(1)}, f32[1,512]{1,0:T(1,128)S(1)}, u32[]{:S(2)}, u32[]{:S(2)}) collective-permute-start(f32[1,512]{1,0:T(1,128)S(1)} %psum.7), channel_id=1, source_target_pairs={{0,64},{64,128},{128,192},{192,0},{1,65},{65,129},{129,193},{193,1... | collective-permute-start | bytes 6152 | tf_op jit(solution)/shard_map/ppermute | solution.py:94
  215.3 4.9 %collective-permute-start.5 = (f32[1,512]{1,0:T(1,128)S(1)}, f32[1,512]{1,0:T(1,128)S(1)}, u32[]{:S(2)}, u32[]{:S(2)}) collective-permute-start(f32[1,512]{1,0:T(1,128)S(1)} %collective-permute-done.4), channel_id=1, source_target_pairs={{0,64},{64,128},{128,192},{192,0},{1,65},{65,129},{129,193},{193,1... | collective-permute-start | bytes 6152 | tf_op jit(solution)/shard_map/ppermute | solution.py:94
  220.2 14.2 %collective-permute-start.6 = (f32[1,512]{1,0:T(1,128)S(1)}, f32[1,512]{1,0:T(1,128)S(1)}, u32[]{:S(2)}, u32[]{:S(2)}) collective-permute-start(f32[1,512]{1,0:T(1,128)S(1)} %collective-permute-done.5), channel_id=1, source_target_pairs={{0,64},{64,128},{128,192},{192,0},{1,65},{65,129},{129,193},{193,1... | collective-permute-start | bytes 6152 | tf_op jit(solution)/shard_map/ppermute | solution.py:94
  224.3 9.3 %copy-start.4 = (f32[1,4,1024]{2,1,0:T(4,128)S(1)}, f32[1,4,1024]{2,1,0:T(4,128)}, u32[]{:S(2)}) copy-start(f32[1,4,1024]{2,1,0:T(4,128)} %param.25) | copy-start | bytes 49156
  224.3 9.4 %copy-start.8 = (s32[64]{0:T(128)S(1)}, s32[64]{0:T(128)}, u32[]{:S(2)}) copy-start(s32[64]{0:T(128)} %param.17) | copy-start | bytes 772
  242.9 12.5 %copy-start.1 = (f32[16,4096]{1,0:T(8,128)S(1)}, f32[16,4096]{1,0:T(8,128)}, u32[]{:S(2)}) copy-start(f32[16,4096]{1,0:T(8,128)} %param.14) | copy-start | bytes 786436
